TPU v7x, 128 devices: a whole 4x4x4 slice. The times are simulated.
128 devices in a mesh: fsdp: 64 (over x, y, z_lo, core), tp: 2 (over z_hi).
Axes of the slice: x: 4, y: 4, z: 4 (z_hi: 2, z_lo: 2; z = z_hi * 2 + z_lo), core: 2. Of those that a mesh axis runs over, the one named last changes fastest.
Arguments:
- inputs: float32 [25600, 768], P(('fsdp', 'tp')), may hold values from -6 to 6
- routes: int32 [25600, 2], P('fsdp'), may hold values from 0 to 15, all different within a row; in each aligned block of 400 rows (0 to 399, 400 to 799, ...) at most 63 rows name the same one
- attention_norm_gain: bfloat16 [768], P('fsdp'), may hold values from 0.099609375 to 1.8984375
- attention_norm_shift: bfloat16 [768], P('fsdp'), may hold values from -3 to 3
- qkv_weight: bfloat16 [3, 768, 768], P(None, 'fsdp', 'tp'), may hold values from -0.21875 to 0.21875
- proj_weight: bfloat16 [768, 768], P('tp', 'fsdp'), may hold values from -0.875 to 0.875
- expert_norm_gain: bfloat16 [768], P('fsdp'), may hold values from 0.099609375 to 1.8984375
- expert_norm_shift: bfloat16 [768], P('fsdp'), may hold values from -3 to 3
- router_weight: bfloat16 [768, 16], P('fsdp'), may hold values from -0.109375 to 0.109375
- expert_in: bfloat16 [768, 16, 3072], P('fsdp', None, 'tp'), may hold values from -0.21875 to 0.21875
- expert_out: bfloat16 [768, 16, 3072], P('fsdp', None, 'tp'), may hold values from -0.4375 to 0.4375
- cotangent: float32 [25600, 768], P(('fsdp', 'tp')), may hold values from -6 to 6
Outputs:
- outputs: float32 [25600, 768], P(('fsdp', 'tp'))
- input_grad: float32 [25600, 768], P(('fsdp', 'tp'))
- attn_gain_grad: float32 [768], P('fsdp')
- attn_shift_grad: float32 [768], P('fsdp')
- qkv_grad: float32 [3, 768, 768], P(None, 'fsdp', 'tp')
- proj_grad: float32 [768, 768], P('tp', 'fsdp')
- moe_gain_grad: float32 [768], P('fsdp')
- moe_shift_grad: float32 [768], P('fsdp')
- router_grad: float32 [768, 16], P('fsdp')
- expert_in_grad: float32 [768, 16, 3072], P('fsdp', None, 'tp')
- expert_out_grad: float32 [768, 16, 3072], P('fsdp', None, 'tp')
Inputs may be any that keep to these rules, and one draw needn't show every extreme that they name: `routes`: in each aligned block of 400 rows (one routing group) the two experts of a row differ and no expert is named by more than 63 rows; some expert is named by exactly 63 rows of some block.
All inputs are finite; a program needn't handle non-finite values.
Results may differ from a plain program's by a relative error of at most 0.01.
Values may be sent and summed in bfloat16 or wider, within the bound.
A program may use at most 192 MiB of HBM per device.

v0:
```python
import jax
import jax.numpy as jnp
from jax import lax
from jax.sharding import PartitionSpec as P

HEAD_DIM = 64
SEQ = 200
REAL_TOK = 197
CAP = 63
EPS = 1e-06
TOP = lax.Precision.HIGHEST


def gelu_exact(value):
    return jax.nn.gelu(value, approximate=False)


def normalize_rows(value, norm_gain, norm_shift):
    row_mean = jnp.mean(value, axis=-1, keepdims=True)
    centered_rows = value - row_mean
    inverse_deviation = lax.rsqrt(
        jnp.mean(centered_rows * centered_rows, axis=-1, keepdims=True) + EPS
    )
    standardized_rows = centered_rows * inverse_deviation
    normed_rows = (
        standardized_rows * norm_gain.astype(jnp.float32) + norm_shift.astype(jnp.float32)
    ).astype(jnp.bfloat16)
    return (normed_rows, standardized_rows, inverse_deviation)


def norm_backward(incoming_gradient, standardized_rows, inverse_deviation, norm_gain):
    scaled_gradient = incoming_gradient * norm_gain.astype(jnp.float32)
    inner_product = (
        scaled_gradient
        - jnp.mean(scaled_gradient, axis=-1, keepdims=True)
        - standardized_rows * jnp.mean(scaled_gradient * standardized_rows, axis=-1, keepdims=True)
    )
    return (
        inverse_deviation * inner_product,
        jnp.sum(incoming_gradient * standardized_rows, axis=0),
        jnp.sum(incoming_gradient, axis=0),
    )


def slot_table(routes, experts, capacity):
    picked = (routes[:, :, None] == jnp.arange(experts, dtype=jnp.int32)[None, None, :]).astype(
        jnp.int32
    )
    flat = picked.reshape(-1, experts)
    before = jnp.cumsum(flat, axis=0) - flat
    number = jnp.sum(before * flat, axis=-1)
    slot = routes.reshape(-1) * capacity + number
    owner = jnp.arange(flat.shape[0], dtype=jnp.int32) // 2
    token_of_slot = jnp.zeros((experts * capacity,), jnp.int32).at[slot].set(owner)
    filled = jnp.zeros((experts * capacity,), jnp.int32).at[slot].set(1)
    return (picked, slot, token_of_slot, filled)


def split_heads(value, images):
    input_rows, width = value.shape
    return value.reshape(images, input_rows // images, width // HEAD_DIM, HEAD_DIM)


def live_keys(length):
    return (jnp.arange(length) < REAL_TOK)[None, None, None, :]


def attend(query, key, value, images):
    query_h = split_heads(query, images)
    key_h = split_heads(key, images)
    value_h = split_heads(value, images)
    scores = jnp.einsum(
        "ishd,ithd->ihst", query_h, key_h, preferred_element_type=jnp.float32
    ) * HEAD_DIM ** (-0.5)
    live = live_keys(scores.shape[-1])
    lse = jnp.log(jnp.sum(jnp.where(live, jnp.exp(scores), 0.0), axis=-1, keepdims=True))
    probs = jnp.where(live, jnp.exp(scores - lse), 0.0).astype(jnp.bfloat16)
    context = jnp.einsum(
        "ihst,ithd->ishd", probs, value_h, preferred_element_type=jnp.float32
    ).astype(jnp.bfloat16)
    return (context.reshape(query.shape), lse)


def attend_back(query, key, value, lse, context_grad, images):
    query_h = split_heads(query, images)
    key_h = split_heads(key, images)
    value_h = split_heads(value, images)
    grad_h = split_heads(context_grad, images)
    scores = jnp.einsum(
        "ishd,ithd->ihst", query_h, key_h, preferred_element_type=jnp.float32
    ) * HEAD_DIM ** (-0.5)
    live = live_keys(scores.shape[-1])
    probs = jnp.where(live, jnp.exp(scores - lse), 0.0)
    value_grad = jnp.einsum(
        "ihst,ishd->ithd", probs.astype(jnp.bfloat16), grad_h, preferred_element_type=jnp.float32
    ).astype(jnp.bfloat16)
    inner_product = jnp.einsum(
        "ishd,ithd->ihst", grad_h, value_h, preferred_element_type=jnp.float32
    )
    score_grad = (
        probs
        * (inner_product - jnp.sum(probs * inner_product, axis=-1, keepdims=True))
        * HEAD_DIM ** (-0.5)
    ).astype(jnp.bfloat16)
    query_grad = jnp.einsum(
        "ihst,ithd->ishd", score_grad, key_h, preferred_element_type=jnp.float32
    ).astype(jnp.bfloat16)
    key_grad = jnp.einsum(
        "ihst,ishd->ithd", score_grad, query_h, preferred_element_type=jnp.float32
    ).astype(jnp.bfloat16)
    shape = query.shape
    return (query_grad.reshape(shape), key_grad.reshape(shape), value_grad.reshape(shape))


def gather_dense(
    qkv_weight,
    proj_weight,
    router_weight,
    attention_norm_gain,
    attention_norm_shift,
    expert_norm_gain,
    expert_norm_shift,
):
    rows = qkv_weight.shape[1]
    heads_width = qkv_weight.shape[2]
    experts = router_weight.shape[1]
    packed = jnp.concatenate(
        [
            jnp.transpose(qkv_weight, (1, 0, 2)).reshape(rows, -1),
            proj_weight.T,
            router_weight,
            jnp.stack(
                [attention_norm_gain, attention_norm_shift, expert_norm_gain, expert_norm_shift],
                axis=1,
            ),
        ],
        axis=1,
    )
    full = lax.all_gather(packed, "fsdp", axis=0, tiled=True)
    width = full.shape[0]
    at = 3 * heads_width
    qkv_full = jnp.transpose(full[:, :at].reshape(width, 3, heads_width), (1, 0, 2))
    proj_full = full[:, at : at + heads_width].T
    at += heads_width
    router_full = full[:, at : at + experts]
    at += experts
    norms = full[:, at : at + 4]
    return (qkv_full, proj_full, router_full, norms[:, 0], norms[:, 1], norms[:, 2], norms[:, 3])


def reduce_dense(qkv_part, proj_part, router_part, norm_parts):
    width = qkv_part.shape[1]
    heads_width = qkv_part.shape[2]
    experts = router_part.shape[1]
    packed = jnp.concatenate(
        [
            jnp.transpose(qkv_part, (1, 0, 2)).reshape(width, -1),
            proj_part.T,
            router_part,
            jnp.stack(norm_parts, axis=1),
        ],
        axis=1,
    )
    part = lax.psum_scatter(packed, "fsdp", scatter_dimension=0, tiled=True)
    rows = part.shape[0]
    at = 3 * heads_width
    qkv_grad = jnp.transpose(part[:, :at].reshape(rows, 3, heads_width), (1, 0, 2))
    proj_grad = part[:, at : at + heads_width].T
    at += heads_width
    shared = lax.psum(part[:, at:], "tp")
    router_grad = shared[:, :experts]
    norm_grads = [shared[:, experts + i] for i in range(len(norm_parts))]
    return (qkv_grad, proj_grad, router_grad, norm_grads)


def group_rows(value):
    return lax.all_gather(value, "tp", axis=0, tiled=True)


def owned_rows(value):
    return lax.psum_scatter(value, "tp", scatter_dimension=0, tiled=True)


def to_owners(slots, holders):
    experts, capacity, width = slots.shape
    spread = jnp.broadcast_to(slots[:, None], (experts, holders, capacity, width)).reshape(
        experts * holders, capacity, width
    )
    moved = lax.all_to_all(spread, "fsdp", split_axis=0, concat_axis=0, tiled=True)
    return moved.reshape(-1, width)


def to_groups(partial_value, experts, holders, capacity):
    width = partial_value.shape[1]
    pieces = partial_value.reshape(experts * holders, capacity, width)
    moved = lax.all_to_all(pieces, "fsdp", split_axis=0, concat_axis=0, tiled=True)
    return jnp.sum(moved.reshape(experts, holders, capacity, width), axis=1)


def per_device(
    inputs,
    routes,
    attention_norm_gain,
    attention_norm_shift,
    qkv_weight,
    proj_weight,
    expert_norm_gain,
    expert_norm_shift,
    router_weight,
    expert_in,
    expert_out,
    cotangent,
):
    f32 = jnp.float32
    bf16 = jnp.bfloat16
    dense = gather_dense(
        qkv_weight,
        proj_weight,
        router_weight,
        attention_norm_gain,
        attention_norm_shift,
        expert_norm_gain,
        expert_norm_shift,
    )
    qkv_full, proj_full, router_full, attention_gain, attention_shift, expert_gain, expert_shift = (
        dense
    )
    group = routes.shape[0]
    images = group // SEQ
    experts = router_full.shape[1]
    width = qkv_full.shape[1]
    units = expert_in.shape[2]
    local_rows = expert_in.shape[0]
    holders = lax.axis_size("fsdp") // experts
    block_units = units // holders
    attention_normed, attention_standardized, attention_inverse_deviation = normalize_rows(
        inputs, attention_gain, attention_shift
    )
    tokens_a = group_rows(attention_normed)
    proj = jnp.einsum("td,idh->ith", tokens_a, qkv_full, preferred_element_type=f32).astype(bf16)
    context, lse = attend(proj[0], proj[1], proj[2], images)
    residual_middle = inputs + owned_rows(jnp.dot(context, proj_full, preferred_element_type=f32))
    expert_normed, expert_standardized, expert_inverse_deviation = normalize_rows(
        residual_middle, expert_gain, expert_shift
    )
    tokens_m = group_rows(expert_normed)
    logits = jnp.dot(tokens_m, router_full, preferred_element_type=f32)
    raised = jnp.exp(logits)
    probs = raised / jnp.sum(raised, axis=-1, keepdims=True)
    picked, slot, token_of_slot, filled = slot_table(routes, experts, CAP)
    gates = jnp.sum(picked.astype(f32) * probs[:, None, :], axis=-1)
    slotted = jnp.where(filled[:, None] > 0, tokens_m[token_of_slot], jnp.zeros((), bf16)).reshape(
        experts, CAP, width
    )
    regroup_in = expert_in.reshape(local_rows, experts * holders, block_units)
    regroup_out = expert_out.reshape(local_rows, experts * holders, block_units)
    own_in, own_out = (
        lax.all_to_all(regroup_in, "fsdp", split_axis=1, concat_axis=0, tiled=True),
        lax.all_to_all(regroup_out, "fsdp", split_axis=1, concat_axis=0, tiled=True),
    )
    own_in = own_in.reshape(width, block_units)
    own_out = own_out.reshape(width, block_units)
    owner_x = to_owners(slotted, holders)
    owner_pre = jnp.dot(owner_x, own_in, preferred_element_type=f32)
    owner_hidden = gelu_exact(owner_pre).astype(bf16)
    owner_res = jnp.einsum("cf,df->cd", owner_hidden, own_out, preferred_element_type=f32)
    expert_res = to_groups(owner_res, experts, holders, CAP)
    routed = expert_res.reshape(experts * CAP, width)[slot].reshape(group, 2, width)
    outputs = residual_middle + owned_rows(jnp.sum(gates[:, :, None] * routed, axis=1))
    qkv_back, proj_back, router_back = (qkv_full, proj_full, router_full)
    attention_gain_gradient, expert_gain_gradient = (attention_gain, expert_gain)
    dout = group_rows(cotangent.astype(bf16))
    dout_f = dout.astype(f32)
    gate_of_slot = jnp.zeros((experts * CAP,), f32).at[slot].set(gates.reshape(-1))
    slot_grad = (
        jnp.where(filled[:, None] > 0, gate_of_slot[:, None] * dout_f[token_of_slot], 0.0)
        .astype(bf16)
        .reshape(experts, CAP, width)
    )
    gate_grad = jnp.sum(dout_f[:, None, :] * routed, axis=-1)
    owner_g = to_owners(slot_grad, holders)
    owner_hgrad = jnp.dot(owner_g, own_out, preferred_element_type=f32)
    owner_pgrad = jax.vjp(gelu_exact, owner_pre)[1](owner_hgrad)[0].astype(bf16)
    owner_back = jnp.einsum("cf,df->cd", owner_pgrad, own_in, preferred_element_type=f32)
    slot_in_grad = to_groups(owner_back, experts, holders, CAP)
    in_local = jnp.einsum("cd,cf->df", owner_x, owner_pgrad, preferred_element_type=f32)
    out_local = jnp.einsum("cd,cf->df", owner_g, owner_hidden, preferred_element_type=f32)
    in_home, out_home = (
        lax.all_to_all(
            in_local.reshape(width, 1, block_units).astype(jnp.bfloat16),
            "fsdp",
            split_axis=0,
            concat_axis=1,
            tiled=True,
        ).astype(jnp.float32),
        lax.all_to_all(
            out_local.reshape(width, 1, block_units).astype(jnp.bfloat16),
            "fsdp",
            split_axis=0,
            concat_axis=1,
            tiled=True,
        ).astype(jnp.float32),
    )
    in_grad = in_home.reshape(local_rows, experts, units)
    out_grad = out_home.reshape(local_rows, experts, units)
    choice_grad = jnp.sum(picked.astype(f32) * gate_grad[:, :, None], axis=1)
    logit_grad = probs * (choice_grad - jnp.sum(probs * choice_grad, axis=-1, keepdims=True))
    router_part = jnp.einsum("td,te->de", tokens_m.astype(f32), logit_grad, precision=TOP)
    routed_in = slot_in_grad.reshape(experts * CAP, width)[slot].reshape(group, 2, width)
    token_gradient = jnp.sum(routed_in, axis=1) + jnp.einsum(
        "te,de->td", logit_grad, router_back.astype(f32), precision=TOP
    )
    expert_norm_backward, expert_gain_partial, expert_shift_partial = norm_backward(
        owned_rows(token_gradient),
        expert_standardized,
        expert_inverse_deviation,
        expert_gain_gradient,
    )
    middle_grad = cotangent + expert_norm_backward
    mid_rows = group_rows(middle_grad.astype(bf16))
    proj_part = jnp.einsum("th,td->hd", context, mid_rows, preferred_element_type=f32)
    context_grad = jnp.einsum("td,hd->th", mid_rows, proj_back, preferred_element_type=f32).astype(
        bf16
    )
    query_grad, key_grad, value_grad = attend_back(
        proj[0], proj[1], proj[2], lse, context_grad, images
    )
    stacked = jnp.stack([query_grad, key_grad, value_grad])
    qkv_part = jnp.einsum("td,ith->idh", tokens_a, stacked, preferred_element_type=f32)
    attention_input_gradient = owned_rows(
        jnp.einsum("ith,idh->td", stacked, qkv_back, preferred_element_type=f32)
    )
    attention_norm_backward, attention_gain_partial, attention_shift_partial = norm_backward(
        attention_input_gradient,
        attention_standardized,
        attention_inverse_deviation,
        attention_gain_gradient,
    )
    input_grad = middle_grad + attention_norm_backward
    qkv_grad, proj_grad, router_grad, norm_grads = reduce_dense(
        qkv_part,
        proj_part,
        router_part,
        [
            attention_gain_partial,
            attention_shift_partial,
            expert_gain_partial,
            expert_shift_partial,
        ],
    )
    return (
        outputs,
        input_grad,
        norm_grads[0],
        norm_grads[1],
        qkv_grad,
        proj_grad,
        norm_grads[2],
        norm_grads[3],
        router_grad,
        in_grad,
        out_grad,
    )


def solution(mesh):
    return jax.shard_map(
        per_device,
        mesh=mesh,
        in_specs=(
            P(("fsdp", "tp"), None),
            P("fsdp", None),
            P("fsdp"),
            P("fsdp"),
            P(None, "fsdp", "tp"),
            P("tp", "fsdp"),
            P("fsdp"),
            P("fsdp"),
            P("fsdp", None),
            P("fsdp", None, "tp"),
            P("fsdp", None, "tp"),
            P(("fsdp", "tp"), None),
        ),
        out_specs=(
            P(("fsdp", "tp"), None),
            P(("fsdp", "tp"), None),
            P("fsdp"),
            P("fsdp"),
            P(None, "fsdp", "tp"),
            P("tp", "fsdp"),
            P("fsdp"),
            P("fsdp"),
            P("fsdp", None),
            P("fsdp", None, "tp"),
            P("fsdp", None, "tp"),
        ),
        check_vma=False,
    )
```

profile of v0, /device:TPU:0, one launch (start us, length us, event | category | flops | bytes accessed | tf_op | source)
XLA Modules:
  0.0 1606.7 jit_solution(12377187689971864063)
XLA Ops:
  15.1 105.2 %all-gather.3.cloned.1.call-done = bf16[64,12,1556]{2,1,0:T(8,128)(2,1)} async-done(((bf16[1,12,1556]{2,1,0:T(8,128)(2,1)}), bf16[64,12,1556]{2,1,0:T(8,128)(2,1)}) %all-gather.3.cloned.1.call-update) | async-done | bytes 2390032 | tf_op jit(solution)/shard_map/all_gather | solution.py:139
  126.7 11.7 all_gather.16
  201.1 9.7 reduce-scatter.5.cloned.1.call-done
  212.3 7.8 all-to-all-start.2
  220.3 19.2 %all_gather.17 = bf16[400,768]{1,0:T(8,128)(2,1)S(1)} all-gather(bf16[200,768]{1,0:T(8,128)(2,1)S(1)} %add_convert_fusion.1), channel_id=1, replica_groups=mesh['fsdp'=64,'tp'=2] {'tp'}, dimensions={0}, use_global_device_ids=true | all-gather | bytes 921600 | tf_op jit(solution)/shard_map/all_gather | solution.py:177
  254.8 6.9 all-to-all-start
  261.8 60.1 %all_gather.18 = bf16[400,768]{1,0:T(8,128)(2,1)S(1)} all-gather(bf16[200,768]{1,0:T(8,128)(2,1)S(1)} %convert_element_type.180), channel_id=1, replica_groups=mesh['fsdp'=64,'tp'=2] {'tp'}, dimensions={0}, use_global_device_ids=true | all-gather | bytes 921600 | tf_op jit(solution)/shard_map/all_gather | solution.py:177
  345.7 25.8 %all-to-all-start.4 = ((bf16[64,63,768]{2,1,0:T(8,128)(2,1)}), bf16[64,63,768]{2,1,0:T(8,128)(2,1)}, u32[]{:S(2)}, u32[]{:S(2)}) async-start(bf16[64,63,768]{2,1,0:T(8,128)(2,1)} %bitcast.138), calls=%async_computation.6 | async-start | bytes 12582912 | tf_op jit(solution)/shard_map/all_to_all | solution.py:189
  372.8 8.5 reshape.285
  381.3 8.8 fusion.111
  390.1 59.2 %all-to-all-done.4 = bf16[64,63,768]{2,1,0:T(8,128)(2,1)} async-done(((bf16[64,63,768]{2,1,0:T(8,128)(2,1)}), bf16[64,63,768]{2,1,0:T(8,128)(2,1)}, u32[]{:S(2)}, u32[]{:S(2)}) %all-to-all-start.4) | async-done | bytes 6193184 | tf_op jit(solution)/shard_map/all_to_all | solution.py:189
  449.3 8.5 reshape.295
  457.9 20.1 %add_convert_fusion = (bf16[4032,384]{1,0:T(8,128)(2,1)}, f32[4032,384]{1,0:T(8,128)}) fusion(f32[4032,384]{1,0:T(8,128)} %fusion.111, bf16[4032,768]{1,0:T(8,128)(2,1)} %reshape.295, bf16[768,384]{1,0:T(8,128)(2,1)S(1)} %reshape.289), kind=kOutput, calls=%fused_computation.13 | convolution fusion | flops 2489647104 | bytes 22265856 | tf_op jit(solution)/shard_map/dot_general | solution.py:282
  482.6 9.8 fusion.113
  492.4 11.1 all-to-all-start.5
  503.7 6.9 multiply_convert_fusion
  515.2 9.9 fusion.112
  525.1 143.2 %all-to-all-done.5 = f32[64,63,768]{2,1,0:T(8,128)} async-done(((f32[64,63,768]{2,1,0:T(8,128)}), f32[64,63,768]{2,1,0:T(8,128)}, u32[]{:S(2)}, u32[]{:S(2)}) %all-to-all-start.5) | async-done | bytes 12386336 | tf_op jit(solution)/shard_map/all_to_all | solution.py:196
  668.3 19.0 %all-to-all-start.3 = ((f32[64,63,768]{2,1,0:T(8,128)}), f32[64,63,768]{2,1,0:T(8,128)}, u32[]{:S(2)}, u32[]{:S(2)}) async-start(f32[64,63,768]{2,1,0:T(8,128)} %fusion.112), calls=%async_computation.4 | async-start | bytes 25165824 | tf_op jit(solution)/shard_map/all_to_all | solution.py:196
  687.4 7.6 bitcast_reduce_fusion
  713.9 138.2 %all-to-all-done.3 = f32[64,63,768]{2,1,0:T(8,128)} async-done(((f32[64,63,768]{2,1,0:T(8,128)}), f32[64,63,768]{2,1,0:T(8,128)}, u32[]{:S(2)}, u32[]{:S(2)}) %all-to-all-start.3) | async-done | bytes 12386336 | tf_op jit(solution)/shard_map/all_to_all | solution.py:196
  852.1 7.7 bitcast_reduce_fusion.1
  873.7 8.1 multiply_reduce_fusion.1
  889.3 33.0 %reduce-scatter.9.cloned.1.call-done = f32[200,768]{1,0:T(8,128)} async-done(((f32[400,768]{1,0:T(8,128)}), f32[200,768]{1,0:T(8,128)}) %reduce-scatter.9.cloned.1.call-update) | async-done | bytes 614416 | tf_op jit(solution)/shard_map/reduce_scatter | solution.py:181
  923.8 26.5 %reduce-scatter.7.cloned.1.call-done = f32[200,768]{1,0:T(8,128)} async-done(((f32[400,768]{1,0:T(8,128)}), f32[200,768]{1,0:T(8,128)}) %reduce-scatter.7.cloned.1.call-update) | async-done | bytes 614416 | tf_op jit(solution)/shard_map/reduce_scatter | solution.py:181
  952.8 11.2 all_gather.19
  1001.9 13.7 reduce-scatter.11.cloned.1.call-done
  1023.5 7.1 fusion.37
  1033.3 7.8 all-to-all-start.6
  1041.1 7.1 fusion.38
  1063.6 9.2 all-to-all-done.7
  1076.9 511.7 %all-reduce.4.cloned.1.call-done = f32[768,1556]{1,0:T(8,128)} async-done(((f32[768,1556]{1,0:T(8,128)}), f32[768,1556]{1,0:T(8,128)}) %all-reduce.4.cloned.1.call-update) | async-done | bytes 4780048
  (246 shorter events, 250.2 us)
Async XLA Ops:
  7.2 113.1 %all-gather.3.cloned.1.call-start = ((), (), s32[]{:S(2)}) async-start(), calls=%async_computation.16 | async-start | bytes 3461120 | tf_op jit(solution)/shard_map/all_gather | solution.py:139
  12.5 198.3 %reduce-scatter.5.cloned.1.call-start = ((), (), s32[]{:S(2)}) async-start(), calls=%async_computation.12 | async-start | bytes 1843200 | tf_op jit(solution)/shard_map/reduce_scatter | solution.py:181
  13.8 151.6 %copy-start.36 = (pred[200]{0:T(512)(128)(4,1)}, pred[200]{0:T(512)(128)(4,1)S(1)}, u32[]{:S(2)}) copy-start(pred[200]{0:T(512)(128)(4,1)S(1)} %iota_compare_fusion.3) | copy-start | bytes 604
  13.8 112.7 %copy-start.27 = (f32[200]{0:T(256)}, f32[200]{0:T(256)S(1)}, u32[]{:S(2)}) copy-start(f32[200]{0:T(256)S(1)} %broadcast_multiply_fusion.6) | copy-start | bytes 2404
  15.1 111.4 %copy-start.31 = (f32[200]{0:T(256)}, f32[200]{0:T(256)S(1)}, u32[]{:S(2)}) copy-start(f32[200]{0:T(256)S(1)} %add_rsqrt_fusion.1) | copy-start | bytes 2404
  124.4 49.6 %copy-start.6 = (bf16[768,1556]{1,0:T(8,128)(2,1)}, bf16[768,1556]{1,0:T(8,128)(2,1)S(1)}, u32[]{:S(2)}) copy-start(bf16[768,1556]{1,0:T(8,128)(2,1)S(1)} %reshape.370) | copy-start | bytes 7170052
  125.0 95.1 %copy-start.24 = (f32[768]{0:T(1024)}, f32[768]{0:T(1024)S(1)}, u32[]{:S(2)}) copy-start(f32[768]{0:T(1024)S(1)} %get-tuple-element.11) | copy-start | bytes 9220
  176.6 22.9 %copy-start.18 = (bf16[12,16,1536]{2,1,0:T(8,128)(2,1)S(1)}, bf16[12,16,1536]{2,1,0:T(8,128)(2,1)}, u32[]{:S(2)}) copy-start(bf16[12,16,1536]{2,1,0:T(8,128)(2,1)} %param.22) | copy-start | bytes 1769476
  179.4 32.9 %all-to-all-start.1 = ((bf16[12,64,384]{2,0,1:T(8,128)(2,1)}), bf16[12,64,384]{2,0,1:T(8,128)(2,1)S(1)}, u32[]{:S(2)}, u32[]{:S(2)}) async-start(bf16[12,64,384]{2,0,1:T(8,128)(2,1)} %copy.285), calls=%async_computation.2 | async-start | bytes 1572864 | tf_op jit(solution)/shard_map/all_to_all | solution.py:258
  212.0 32.7 %copy-start.4 = (f32[200,768]{1,0:T(8,128)}, f32[200,768]{1,0:T(8,128)S(1)}, u32[]{:S(2)}) copy-start(f32[200,768]{1,0:T(8,128)S(1)} %get-tuple-element.34) | copy-start | bytes 1843204
  212.0 32.7 %copy-start.29 = (f32[200]{0:T(256)}, f32[200]{0:T(256)S(1)}, u32[]{:S(2)}) copy-start(f32[200]{0:T(256)S(1)} %broadcast_multiply_fusion.5) | copy-start | bytes 2404
  212.3 32.4 %copy-start.33 = (f32[200]{0:T(256)}, f32[200]{0:T(256)S(1)}, u32[]{:S(2)}) copy-start(f32[200]{0:T(256)S(1)} %add_rsqrt_fusion) | copy-start | bytes 2404
  212.3 37.7 %all-to-all-start.2 = ((bf16[12,64,384]{2,0,1:T(8,128)(2,1)}), bf16[12,64,384]{2,0,1:T(8,128)(2,1)S(1)}, u32[]{:S(2)}, u32[]{:S(2)}) async-start(bf16[12,64,384]{2,0,1:T(8,128)(2,1)} %copy.286), calls=%async_computation.3 | async-start | bytes 1572864 | tf_op jit(solution)/shard_map/all_to_all | solution.py:259
  239.5 91.0 %copy-start = (bf16[400,768]{1,0:T(8,128)(2,1)}, bf16[400,768]{1,0:T(8,128)(2,1)S(1)}, u32[]{:S(2)}) copy-start(bf16[400,768]{1,0:T(8,128)(2,1)S(1)} %all_gather.17) | copy-start | bytes 1843204
  254.8 86.1 %all-to-all-start = ((bf16[64,63,768]{2,1,0:T(8,128)(2,1)}), bf16[64,63,768]{2,1,0:T(8,128)(2,1)}, u32[]{:S(2)}, u32[]{:S(2)}) async-start(bf16[64,63,768]{2,1,0:T(8,128)(2,1)} %bitcast.137), calls=%async_computation.1 | async-start | bytes 12582912 | tf_op jit(solution)/shard_map/all_to_all | solution.py:189
  345.7 103.6 %all-to-all-start.4 = ((bf16[64,63,768]{2,1,0:T(8,128)(2,1)}), bf16[64,63,768]{2,1,0:T(8,128)(2,1)}, u32[]{:S(2)}, u32[]{:S(2)}) async-start(bf16[64,63,768]{2,1,0:T(8,128)(2,1)} %bitcast.138), calls=%async_computation.6 | async-start | bytes 12582912 | tf_op jit(solution)/shard_map/all_to_all | solution.py:189
  492.4 175.9 %all-to-all-start.5 = ((f32[64,63,768]{2,1,0:T(8,128)}), f32[64,63,768]{2,1,0:T(8,128)}, u32[]{:S(2)}, u32[]{:S(2)}) async-start(f32[64,63,768]{2,1,0:T(8,128)} %fusion.113), calls=%async_computation.7 | async-start | bytes 25165824 | tf_op jit(solution)/shard_map/all_to_all | solution.py:196
  668.3 183.8 %all-to-all-start.3 = ((f32[64,63,768]{2,1,0:T(8,128)}), f32[64,63,768]{2,1,0:T(8,128)}, u32[]{:S(2)}, u32[]{:S(2)}) async-start(f32[64,63,768]{2,1,0:T(8,128)} %fusion.112), calls=%async_computation.4 | async-start | bytes 25165824 | tf_op jit(solution)/shard_map/all_to_all | solution.py:196
  687.3 235.0 %reduce-scatter.9.cloned.1.call-start = ((), (), s32[]{:S(2)}) async-start(), calls=%async_computation.14 | async-start | bytes 1843200 | tf_op jit(solution)/shard_map/reduce_scatter | solution.py:181
  885.5 64.8 %reduce-scatter.7.cloned.1.call-start = ((), (), s32[]{:S(2)}) async-start(), calls=%async_computation.13 | async-start | bytes 1843200 | tf_op jit(solution)/shard_map/reduce_scatter | solution.py:181
  886.1 36.3 %copy-start.5 = (f32[200,768]{1,0:T(8,128)S(1)}, f32[200,768]{1,0:T(8,128)}, u32[]{:S(2)}) copy-start(f32[200,768]{1,0:T(8,128)} %copy-done.4) | copy-start | bytes 1843204
  886.1 36.2 %copy-start.25 = (f32[768]{0:T(1024)S(1)}, f32[768]{0:T(1024)}, u32[]{:S(2)}) copy-start(f32[768]{0:T(1024)} %copy-done.24) | copy-start | bytes 9220
  886.1 36.2 %copy-start.30 = (f32[200]{0:T(256)S(1)}, f32[200]{0:T(256)}, u32[]{:S(2)}) copy-start(f32[200]{0:T(256)} %copy-done.29) | copy-start | bytes 2404
  886.1 36.2 %copy-start.34 = (f32[200]{0:T(256)S(1)}, f32[200]{0:T(256)}, u32[]{:S(2)}) copy-start(f32[200]{0:T(256)} %copy-done.33) | copy-start | bytes 2404
  886.1 64.2 %copy-start.9 = (f32[200,768]{1,0:T(8,128)S(1)}, f32[200,768]{1,0:T(8,128)}, u32[]{:S(2)}) copy-start(f32[200,768]{1,0:T(8,128)} %param.23) | copy-start | bytes 1843204
  886.2 129.5 %reduce-scatter.11.cloned.1.call-start = ((), (), s32[]{:S(2)}) async-start(), calls=%async_computation.15 | async-start | bytes 1843200 | tf_op jit(solution)/shard_map/reduce_scatter | solution.py:181
  989.8 598.8 %all-reduce.4.cloned.1.call-start = ((), (), s32[]{:S(2)}) async-start(), calls=%async_computation.17 | async-start | bytes 10223616
  995.9 19.7 %copy-start.3 = (f32[200,768]{1,0:T(8,128)S(1)}, f32[200,768]{1,0:T(8,128)}, u32[]{:S(2)}) copy-start(f32[200,768]{1,0:T(8,128)} %param.12) | copy-start | bytes 1843204
  995.9 19.7 %copy-start.23 = (f32[768]{0:T(1024)S(1)}, f32[768]{0:T(1024)}, u32[]{:S(2)}) copy-start(f32[768]{0:T(1024)} %copy-done.22) | copy-start | bytes 9220
  995.9 19.7 %copy-start.28 = (f32[200]{0:T(256)S(1)}, f32[200]{0:T(256)}, u32[]{:S(2)}) copy-start(f32[200]{0:T(256)} %copy-done.27) | copy-start | bytes 2404
  1033.3 21.2 %all-to-all-start.6 = ((bf16[64,2,2304]{2,1,0:T(2,128)(2,1)}), bf16[64,2,2304]{2,1,0:T(2,128)(2,1)S(1)}, u32[]{:S(2)}, u32[]{:S(2)}) async-start(bf16[64,2,2304]{2,1,0:T(2,128)(2,1)} %reshape.401), calls=%async_computation.10 | async-start | bytes 1179648 | tf_op jit(solution)/shard_map/all_to_all | solution.py:289
  1054.5 18.3 %all-to-all-start.7 = ((bf16[64,2,2304]{2,1,0:T(2,128)(2,1)}), bf16[64,2,2304]{2,1,0:T(2,128)(2,1)S(1)}, u32[]{:S(2)}, u32[]{:S(2)}) async-start(bf16[64,2,2304]{2,1,0:T(2,128)(2,1)} %reshape.403), calls=%async_computation.11 | async-start | bytes 1179648 | tf_op jit(solution)/shard_map/all_to_all | solution.py:296
  (20 other events, 122.3 us)
Sparse Core Ops, SparseCore 0:
  12.6 107.5 all-gather.2
  176.7 34.0 reduce-scatter.4
  885.6 36.6 reduce-scatter.8
  924.6 25.6 reduce-scatter.6
  989.9 25.6 reduce-scatter.10
  1023.7 564.9 all-reduce.3
where the time goes:
time: 1620 us; the launch traced here: 1610 us
  waiting for transfers between devices  1050 us (65%)
  local copies, waits for them, and re-layouts  171 us (11%)
  blocking collectives  109 us (7%)
  matrix products  106 us (7%)
  starting transfers between devices  90.5 us (6%)
  other arithmetic  60.1 us (4%)
    unnamed x7, waiting for transfers between devices  512 us
    all_to_all x2, waiting for transfers between devices, to_groups(): lax.all_to_all(pieces, 'fsdp', split_axis=0, concat_axis=0, tiled=True)  281 us
    all_gather x1, waiting for transfers between devices, gather_dense(): full = lax.all_gather(packed, 'fsdp', axis=0, tiled=True)  105 us
    all_gather x4, blocking collectives, group_rows(): return lax.all_gather(value, 'tp', axis=0, tiled=True)  102 us
    reduce_scatter x4, waiting for transfers between devices, owned_rows(): return lax.psum_scatter(value, 'tp', scatter_dimension=0, tiled=True)  83 us
    all_to_all x2, waiting for transfers between devices, to_owners(): lax.all_to_all(spread, 'fsdp', split_axis=0, concat_axis=0, tiled=True)  59.2 us
    all_to_all x2, starting transfers between devices, to_owners(): lax.all_to_all(spread, 'fsdp', split_axis=0, concat_axis=0, tiled=True)  32.8 us
  transfers between devices with their start and end apart: 14, of which 11 were waited for; matrix products, arithmetic and copies ran while one was open for 10% of the time, Pallas kernels for 0%

commit v1 on v0

--- a/solution.py
+++ b/solution.py
@@ -136,7 +136,9 @@
         ],
         axis=1,
     )
-    full = lax.all_gather(packed, "fsdp", axis=0, tiled=True)
+    full = jnp.concatenate(
+        jax.lax.all_to_all(jnp.stack(jax.lax.axis_size("fsdp") * [packed], axis=0), "fsdp", 0, 0), 0
+    )
     width = full.shape[0]
     at = 3 * heads_width
     qkv_full = jnp.transpose(full[:, :at].reshape(width, 3, heads_width), (1, 0, 2))

time: 1620 us -> 1570 us (0.969)
  waiting for transfers between devices: 1050 us -> 992 us
    all_gather x1 -> x0, waiting for transfers between devices: 105 us -> none  [gather_dense(): full = lax.all_gather(packed, 'fsdp', axis=0, tiled=True)]
    all_to_all x0 -> x1, waiting for transfers between devices: none -> 42 us  [gather_dense(): jax.lax.all_to_all(jnp.stack(jax.lax.axis_size('fsdp') * [packed], axis=0...]
    unnamed x7 -> x6, waiting for transfers between devices: 512 us -> 512 us
where the time goes in v1:
time: 1570 us; the launch traced here: 1550 us
  waiting for transfers between devices  992 us (63%)
  local copies, waits for them, and re-layouts  172 us (11%)
  blocking collectives  109 us (7%)
  matrix products  106 us (7%)
  starting transfers between devices  101 us (6%)
  other arithmetic  57.9 us (4%)
    unnamed x6, waiting for transfers between devices  512 us
    all_to_all x2, waiting for transfers between devices, to_groups(): lax.all_to_all(pieces, 'fsdp', split_axis=0, concat_axis=0, tiled=True)  281 us
    all_gather x4, blocking collectives, group_rows(): return lax.all_gather(value, 'tp', axis=0, tiled=True)  103 us
    reduce_scatter x4, waiting for transfers between devices, owned_rows(): return lax.psum_scatter(value, 'tp', scatter_dimension=0, tiled=True)  83.6 us
    all_to_all x2, waiting for transfers between devices, to_owners(): lax.all_to_all(spread, 'fsdp', split_axis=0, concat_axis=0, tiled=True)  59.2 us
    all_to_all x1, waiting for transfers between devices, gather_dense(): jax.lax.all_to_all(jnp.stack(jax.lax.axis_size('fsdp') * [packed], axis=0...  42 us
    all_to_all x2, starting transfers between devices, to_owners(): lax.all_to_all(spread, 'fsdp', split_axis=0, concat_axis=0, tiled=True)  32.7 us
  transfers between devices with their start and end apart: 14, of which 11 were waited for; matrix products, arithmetic and copies ran while one was open for 10% of the time, Pallas kernels for 0%

profile of v1, /device:TPU:0, one launch (start us, length us, event | category | flops | bytes accessed | tf_op | source)
XLA Modules:
  0.0 1554.4 jit_solution(6359766206836870252)
XLA Ops:
  13.8 9.7 all-to-all-start
  24.1 42.0 %all-to-all-done = bf16[64,12,1556]{2,1,0:T(8,128)(2,1)} async-done(((bf16[64,12,1556]{2,1,0:T(8,128)(2,1)}), bf16[64,12,1556]{2,1,0:T(8,128)(2,1)}, u32[]{:S(2)}, u32[]{:S(2)}) %all-to-all-start) | async-done | bytes 2390048 | tf_op jit(solution)/shard_map/all_to_all | solution.py:140
  72.5 12.4 all_gather.12
  125.8 6.9 all-to-all-start.2
  148.2 10.4 reduce-scatter.5.cloned.1.call-done
  160.0 7.8 all-to-all-start.3
  168.1 19.2 %all_gather.13 = bf16[400,768]{1,0:T(8,128)(2,1)S(1)} all-gather(bf16[200,768]{1,0:T(8,128)(2,1)S(1)} %add_convert_fusion.1), channel_id=1, replica_groups=mesh['fsdp'=64,'tp'=2] {'tp'}, dimensions={0}, use_global_device_ids=true | all-gather | bytes 921600 | tf_op jit(solution)/shard_map/all_gather | solution.py:179
  209.6 60.1 %all_gather.14 = bf16[400,768]{1,0:T(8,128)(2,1)S(1)} all-gather(bf16[200,768]{1,0:T(8,128)(2,1)S(1)} %convert_element_type.180), channel_id=1, replica_groups=mesh['fsdp'=64,'tp'=2] {'tp'}, dimensions={0}, use_global_device_ids=true | all-gather | bytes 921600 | tf_op jit(solution)/shard_map/all_gather | solution.py:179
  293.5 25.8 %all-to-all-start.5 = ((bf16[64,63,768]{2,1,0:T(8,128)(2,1)}), bf16[64,63,768]{2,1,0:T(8,128)(2,1)}, u32[]{:S(2)}, u32[]{:S(2)}) async-start(bf16[64,63,768]{2,1,0:T(8,128)(2,1)} %bitcast.137), calls=%async_computation.7 | async-start | bytes 12582912 | tf_op jit(solution)/shard_map/all_to_all | solution.py:191
  320.5 8.5 reshape.291
  329.0 8.8 fusion.111
  337.9 59.2 %all-to-all-done.5 = bf16[64,63,768]{2,1,0:T(8,128)(2,1)} async-done(((bf16[64,63,768]{2,1,0:T(8,128)(2,1)}), bf16[64,63,768]{2,1,0:T(8,128)(2,1)}, u32[]{:S(2)}, u32[]{:S(2)}) %all-to-all-start.5) | async-done | bytes 6193184 | tf_op jit(solution)/shard_map/all_to_all | solution.py:191
  397.1 8.5 reshape.301
  405.7 20.1 %add_convert_fusion = (bf16[4032,384]{1,0:T(8,128)(2,1)}, f32[4032,384]{1,0:T(8,128)}) fusion(f32[4032,384]{1,0:T(8,128)} %fusion.111, bf16[4032,768]{1,0:T(8,128)(2,1)} %reshape.301, bf16[768,384]{1,0:T(8,128)(2,1)S(1)} %reshape.295), kind=kOutput, calls=%fused_computation.13 | convolution fusion | flops 2489647104 | bytes 22265856 | tf_op jit(solution)/shard_map/dot_general | solution.py:284
  430.4 9.8 fusion.113
  440.2 11.1 all-to-all-start.6
  462.9 9.9 fusion.112
  472.8 143.2 %all-to-all-done.6 = f32[64,63,768]{2,1,0:T(8,128)} async-done(((f32[64,63,768]{2,1,0:T(8,128)}), f32[64,63,768]{2,1,0:T(8,128)}, u32[]{:S(2)}, u32[]{:S(2)}) %all-to-all-start.6) | async-done | bytes 12386336 | tf_op jit(solution)/shard_map/all_to_all | solution.py:198
  616.1 19.0 %all-to-all-start.4 = ((f32[64,63,768]{2,1,0:T(8,128)}), f32[64,63,768]{2,1,0:T(8,128)}, u32[]{:S(2)}, u32[]{:S(2)}) async-start(f32[64,63,768]{2,1,0:T(8,128)} %fusion.112), calls=%async_computation.5 | async-start | bytes 25165824 | tf_op jit(solution)/shard_map/all_to_all | solution.py:198
  635.2 7.6 bitcast_reduce_fusion
  661.6 138.2 %all-to-all-done.4 = f32[64,63,768]{2,1,0:T(8,128)} async-done(((f32[64,63,768]{2,1,0:T(8,128)}), f32[64,63,768]{2,1,0:T(8,128)}, u32[]{:S(2)}, u32[]{:S(2)}) %all-to-all-start.4) | async-done | bytes 12386336 | tf_op jit(solution)/shard_map/all_to_all | solution.py:198
  799.9 7.7 bitcast_reduce_fusion.1
  821.5 8.1 multiply_reduce_fusion.1
  837.2 32.9 %reduce-scatter.9.cloned.1.call-done = f32[200,768]{1,0:T(8,128)} async-done(((f32[400,768]{1,0:T(8,128)}), f32[200,768]{1,0:T(8,128)}) %reduce-scatter.9.cloned.1.call-update) | async-done | bytes 614416 | tf_op jit(solution)/shard_map/reduce_scatter | solution.py:183
  871.6 26.6 %reduce-scatter.7.cloned.1.call-done = f32[200,768]{1,0:T(8,128)} async-done(((f32[400,768]{1,0:T(8,128)}), f32[200,768]{1,0:T(8,128)}) %reduce-scatter.7.cloned.1.call-update) | async-done | bytes 614416 | tf_op jit(solution)/shard_map/reduce_scatter | solution.py:183
  900.7 11.2 all_gather.15
  949.8 13.8 reduce-scatter.11.cloned.1.call-done
  971.5 7.1 fusion.37
  981.2 7.8 all-to-all-start.7
  989.0 7.1 fusion.38
  1011.6 9.2 all-to-all-done.8
  1024.9 511.7 %all-reduce.4.cloned.1.call-done = f32[768,1556]{1,0:T(8,128)} async-done(((f32[768,1556]{1,0:T(8,128)}), f32[768,1556]{1,0:T(8,128)}) %all-reduce.4.cloned.1.call-update) | async-done | bytes 4780048
  (246 shorter events, 257.2 us)
Async XLA Ops:
  13.8 52.2 %all-to-all-start = ((bf16[64,12,1556]{2,1,0:T(8,128)(2,1)}), bf16[64,12,1556]{2,1,0:T(8,128)(2,1)}, u32[]{:S(2)}, u32[]{:S(2)}) async-start(bf16[64,12,1556]{2,1,0:T(8,128)(2,1)} %stack.24), calls=%async_computation | async-start | bytes 6815744 | tf_op jit(solution)/shard_map/all_to_all | solution.py:140
  23.6 135.0 %reduce-scatter.5.cloned.1.call-start = ((), (), s32[]{:S(2)}) async-start(), calls=%async_computation.13 | async-start | bytes 1843200 | tf_op jit(solution)/shard_map/reduce_scatter | solution.py:183
  23.8 88.1 %copy-start.36 = (pred[200]{0:T(512)(128)(4,1)}, pred[200]{0:T(512)(128)(4,1)S(1)}, u32[]{:S(2)}) copy-start(pred[200]{0:T(512)(128)(4,1)S(1)} %iota_compare_fusion.3) | copy-start | bytes 604
  23.8 48.5 %copy-start.27 = (f32[200]{0:T(256)}, f32[200]{0:T(256)S(1)}, u32[]{:S(2)}) copy-start(f32[200]{0:T(256)S(1)} %broadcast_multiply_fusion.6) | copy-start | bytes 2404
  24.0 48.2 %copy-start.31 = (f32[200]{0:T(256)}, f32[200]{0:T(256)S(1)}, u32[]{:S(2)}) copy-start(f32[200]{0:T(256)S(1)} %add_rsqrt_fusion.1) | copy-start | bytes 2404
  70.2 50.2 %copy-start.6 = (bf16[768,1556]{1,0:T(8,128)(2,1)}, bf16[768,1556]{1,0:T(8,128)(2,1)S(1)}, u32[]{:S(2)}) copy-start(bf16[768,1556]{1,0:T(8,128)(2,1)S(1)} %reshape.285) | copy-start | bytes 7170052
  70.8 97.1 %copy-start.24 = (f32[768]{0:T(1024)}, f32[768]{0:T(1024)S(1)}, u32[]{:S(2)}) copy-start(f32[768]{0:T(1024)S(1)} %get-tuple-element.11) | copy-start | bytes 9220
  123.0 23.6 %copy-start.18 = (bf16[12,16,1536]{2,1,0:T(8,128)(2,1)S(1)}, bf16[12,16,1536]{2,1,0:T(8,128)(2,1)}, u32[]{:S(2)}) copy-start(bf16[12,16,1536]{2,1,0:T(8,128)(2,1)} %param.22) | copy-start | bytes 1769476
  125.8 34.2 %all-to-all-start.2 = ((bf16[12,64,384]{2,0,1:T(8,128)(2,1)}), bf16[12,64,384]{2,0,1:T(8,128)(2,1)S(1)}, u32[]{:S(2)}, u32[]{:S(2)}) async-start(bf16[12,64,384]{2,0,1:T(8,128)(2,1)} %copy.285), calls=%async_computation.3 | async-start | bytes 1572864 | tf_op jit(solution)/shard_map/all_to_all | solution.py:260
  159.8 32.7 %copy-start.4 = (f32[200,768]{1,0:T(8,128)}, f32[200,768]{1,0:T(8,128)S(1)}, u32[]{:S(2)}) copy-start(f32[200,768]{1,0:T(8,128)S(1)} %get-tuple-element.34) | copy-start | bytes 1843204
  159.8 32.7 %copy-start.29 = (f32[200]{0:T(256)}, f32[200]{0:T(256)S(1)}, u32[]{:S(2)}) copy-start(f32[200]{0:T(256)S(1)} %broadcast_multiply_fusion.5) | copy-start | bytes 2404
  160.0 32.4 %copy-start.33 = (f32[200]{0:T(256)}, f32[200]{0:T(256)S(1)}, u32[]{:S(2)}) copy-start(f32[200]{0:T(256)S(1)} %add_rsqrt_fusion) | copy-start | bytes 2404
  160.0 37.7 %all-to-all-start.3 = ((bf16[12,64,384]{2,0,1:T(8,128)(2,1)}), bf16[12,64,384]{2,0,1:T(8,128)(2,1)S(1)}, u32[]{:S(2)}, u32[]{:S(2)}) async-start(bf16[12,64,384]{2,0,1:T(8,128)(2,1)} %copy.286), calls=%async_computation.4 | async-start | bytes 1572864 | tf_op jit(solution)/shard_map/all_to_all | solution.py:261
  187.2 91.0 %copy-start = (bf16[400,768]{1,0:T(8,128)(2,1)}, bf16[400,768]{1,0:T(8,128)(2,1)S(1)}, u32[]{:S(2)}) copy-start(bf16[400,768]{1,0:T(8,128)(2,1)S(1)} %all_gather.13) | copy-start | bytes 1843204
  202.6 86.1 %all-to-all-start.1 = ((bf16[64,63,768]{2,1,0:T(8,128)(2,1)}), bf16[64,63,768]{2,1,0:T(8,128)(2,1)}, u32[]{:S(2)}, u32[]{:S(2)}) async-start(bf16[64,63,768]{2,1,0:T(8,128)(2,1)} %bitcast.136), calls=%async_computation.2 | async-start | bytes 12582912 | tf_op jit(solution)/shard_map/all_to_all | solution.py:191
  293.5 103.6 %all-to-all-start.5 = ((bf16[64,63,768]{2,1,0:T(8,128)(2,1)}), bf16[64,63,768]{2,1,0:T(8,128)(2,1)}, u32[]{:S(2)}, u32[]{:S(2)}) async-start(bf16[64,63,768]{2,1,0:T(8,128)(2,1)} %bitcast.137), calls=%async_computation.7 | async-start | bytes 12582912 | tf_op jit(solution)/shard_map/all_to_all | solution.py:191
  440.2 175.9 %all-to-all-start.6 = ((f32[64,63,768]{2,1,0:T(8,128)}), f32[64,63,768]{2,1,0:T(8,128)}, u32[]{:S(2)}, u32[]{:S(2)}) async-start(f32[64,63,768]{2,1,0:T(8,128)} %fusion.113), calls=%async_computation.8 | async-start | bytes 25165824 | tf_op jit(solution)/shard_map/all_to_all | solution.py:198
  616.1 183.8 %all-to-all-start.4 = ((f32[64,63,768]{2,1,0:T(8,128)}), f32[64,63,768]{2,1,0:T(8,128)}, u32[]{:S(2)}, u32[]{:S(2)}) async-start(f32[64,63,768]{2,1,0:T(8,128)} %fusion.112), calls=%async_computation.5 | async-start | bytes 25165824 | tf_op jit(solution)/shard_map/all_to_all | solution.py:198
  635.1 235.0 %reduce-scatter.9.cloned.1.call-start = ((), (), s32[]{:S(2)}) async-start(), calls=%async_computation.15 | async-start | bytes 1843200 | tf_op jit(solution)/shard_map/reduce_scatter | solution.py:183
  833.3 64.9 %reduce-scatter.7.cloned.1.call-start = ((), (), s32[]{:S(2)}) async-start(), calls=%async_computation.14 | async-start | bytes 1843200 | tf_op jit(solution)/shard_map/reduce_scatter | solution.py:183
  834.0 36.1 %copy-start.5 = (f32[200,768]{1,0:T(8,128)S(1)}, f32[200,768]{1,0:T(8,128)}, u32[]{:S(2)}) copy-start(f32[200,768]{1,0:T(8,128)} %copy-done.4) | copy-start | bytes 1843204
  834.0 36.1 %copy-start.25 = (f32[768]{0:T(1024)S(1)}, f32[768]{0:T(1024)}, u32[]{:S(2)}) copy-start(f32[768]{0:T(1024)} %copy-done.24) | copy-start | bytes 9220
  834.1 36.1 %copy-start.30 = (f32[200]{0:T(256)S(1)}, f32[200]{0:T(256)}, u32[]{:S(2)}) copy-start(f32[200]{0:T(256)} %copy-done.29) | copy-start | bytes 2404
  834.1 36.1 %copy-start.34 = (f32[200]{0:T(256)S(1)}, f32[200]{0:T(256)}, u32[]{:S(2)}) copy-start(f32[200]{0:T(256)} %copy-done.33) | copy-start | bytes 2404
  834.1 64.1 %copy-start.9 = (f32[200,768]{1,0:T(8,128)S(1)}, f32[200,768]{1,0:T(8,128)}, u32[]{:S(2)}) copy-start(f32[200,768]{1,0:T(8,128)} %param.23) | copy-start | bytes 1843204
  834.1 129.4 %reduce-scatter.11.cloned.1.call-start = ((), (), s32[]{:S(2)}) async-start(), calls=%async_computation.16 | async-start | bytes 1843200 | tf_op jit(solution)/shard_map/reduce_scatter | solution.py:183
  937.7 598.9 %all-reduce.4.cloned.1.call-start = ((), (), s32[]{:S(2)}) async-start(), calls=%async_computation.17 | async-start | bytes 10223616
  943.8 19.7 %copy-start.3 = (f32[200,768]{1,0:T(8,128)S(1)}, f32[200,768]{1,0:T(8,128)}, u32[]{:S(2)}) copy-start(f32[200,768]{1,0:T(8,128)} %param.12) | copy-start | bytes 1843204
  943.8 19.7 %copy-start.23 = (f32[768]{0:T(1024)S(1)}, f32[768]{0:T(1024)}, u32[]{:S(2)}) copy-start(f32[768]{0:T(1024)} %copy-done.22) | copy-start | bytes 9220
  943.8 19.7 %copy-start.28 = (f32[200]{0:T(256)S(1)}, f32[200]{0:T(256)}, u32[]{:S(2)}) copy-start(f32[200]{0:T(256)} %copy-done.27) | copy-start | bytes 2404
  981.2 21.1 %all-to-all-start.7 = ((bf16[64,2,2304]{2,1,0:T(2,128)(2,1)}), bf16[64,2,2304]{2,1,0:T(2,128)(2,1)S(1)}, u32[]{:S(2)}, u32[]{:S(2)}) async-start(bf16[64,2,2304]{2,1,0:T(2,128)(2,1)} %reshape.405), calls=%async_computation.11 | async-start | bytes 1179648 | tf_op jit(solution)/shard_map/all_to_all | solution.py:291
  1002.3 18.4 %all-to-all-start.8 = ((bf16[64,2,2304]{2,1,0:T(2,128)(2,1)}), bf16[64,2,2304]{2,1,0:T(2,128)(2,1)S(1)}, u32[]{:S(2)}, u32[]{:S(2)}) async-start(bf16[64,2,2304]{2,1,0:T(2,128)(2,1)} %reshape.407), calls=%async_computation.12 | async-start | bytes 1179648 | tf_op jit(solution)/shard_map/all_to_all | solution.py:298
  (20 other events, 131.2 us)
Sparse Core Ops, SparseCore 0:
  123.2 35.3 reduce-scatter.4
  833.4 36.6 reduce-scatter.8
  872.5 25.6 reduce-scatter.6
  937.8 25.6 reduce-scatter.10
  971.6 564.9 all-reduce.3
